TPU v7x, 32 devices: a whole 2x2x4 slice. The times are simulated.
32 devices in a mesh: group: 2 (over y), section: 4 (over z), tensor: 4 (over x, core).
Axes of the slice: x: 2, y: 2, z: 4, core: 2. Of those that a mesh axis runs over, the one named last changes fastest.
Arguments:
- inputs: bfloat16 [48, 4096], P('group', 'tensor'), parts along dimension 0, may hold values from -6 to 6
- gains: float32 [4, 4096], P('section'), may hold values from 0.5 to 1.5
- w_query: bfloat16 [4, 4096, 4096], P('section', None, 'tensor'), may hold values from -0.09375 to 0.09375
- w_key: bfloat16 [4, 4096, 1024], P('section', None, 'tensor'), may hold values from -0.09375 to 0.09375
- w_value: bfloat16 [4, 4096, 1024], P('section', None, 'tensor'), may hold values from -0.09375 to 0.09375
- w_out: bfloat16 [4, 4096, 4096], P('section', 'tensor'), may hold values from -0.375 to 0.375
- key_cache: bfloat16 [4, 48, 128, 1024], P('section', 'group', None, 'tensor'), parts along dimension 1, may hold values from -64 to 64
- value_cache: bfloat16 [4, 48, 128, 1024], P('section', 'group', None, 'tensor'), parts along dimension 1, may hold values from -6 to 6
- cache_lens: int32 [48], P('group'), parts along dimension 0, may hold values from 1 to 128, as said below
- exit_plan: int32 [48], P('group'), parts along dimension 0, may hold values from 1 to 4, as said below
Outputs:
- section_hidden: bfloat16 [4, 48, 4096], P('section', 'group', 'tensor'), parts along dimension 1
- new_keys: bfloat16 [4, 48, 1024], P('section', 'group', 'tensor'), parts along dimension 1
- new_values: bfloat16 [4, 48, 1024], P('section', 'group', 'tensor'), parts along dimension 1
There are 2 independent parts, one for each index of `group`. A program takes and returns all parts, laid end to end along the dimension named above; an argument that names none is the same for every part. Nothing has to cross between parts.
Inputs may be any that keep to these rules, and one draw needn't show every extreme that they name: Cached slots 0 to cache_lens - 1 of a row are live; some row has exactly 128. `exit_plan`: some row runs all 4 layers in full.
All inputs are finite; a program needn't handle non-finite values.
Results may differ from a plain program's by a relative error of at most 0.022.
The roundings to bfloat16 on the way count: a program that leaves them out, or rounds other values in their place, can miss the bound.
Values may be sent and summed in bfloat16 or wider, within the bound.
A program may use at most 128 MiB of HBM per device.

v0:
```python
import math

import jax
import jax.numpy as jnp
from jax import lax
from jax.sharding import PartitionSpec as P

HEAD_DIM = 128


NORM_EPSILON = 1e-05
ROPE_BASE = 500000.0
MASKED_SCORE = -1e30


def shifted(value, axis, steps):
    count = lax.axis_size(axis)
    leading, last = (max(0, -steps), min(count, count - steps))
    return lax.ppermute(value, axis, [(source, source + steps) for source in range(leading, last)])


def rotate(vectors, positions):
    half_dim = vectors.shape[-1] // 2
    frequency = ROPE_BASE ** (-(jnp.arange(half_dim, dtype=jnp.float32) * 2.0 / vectors.shape[-1]))
    angles = positions.astype(jnp.float32)[:, None, None] * frequency[None, None, :]
    cos_part = jnp.cos(angles)
    sin_part = jnp.sin(angles)
    lower_half = vectors[..., :half_dim]
    upper_half = vectors[..., half_dim:]
    return jnp.concatenate(
        [
            lower_half * cos_part - upper_half * sin_part,
            upper_half * cos_part + lower_half * sin_part,
        ],
        axis=-1,
    )


def attend(
    normed, lengths, query_weight, key_weight, value_weight, keys_cached, values_cached, kv_local
):
    row_count = normed.shape[0]
    cache_slots = keys_cached.shape[1]
    per_kv = query_weight.shape[1] // (kv_local * HEAD_DIM)
    inv_root = 1.0 / math.sqrt(HEAD_DIM)
    queries = jnp.dot(normed, query_weight, preferred_element_type=jnp.float32).reshape(
        row_count, kv_local * per_kv, HEAD_DIM
    )
    queries = (
        rotate(queries, lengths).astype(jnp.bfloat16).reshape(row_count, kv_local, per_kv, HEAD_DIM)
    )
    key_new = jnp.dot(normed, key_weight, preferred_element_type=jnp.float32).reshape(
        row_count, kv_local, HEAD_DIM
    )
    key_new = rotate(key_new, lengths).astype(jnp.bfloat16)
    value_new = (
        jnp.dot(normed, value_weight, preferred_element_type=jnp.float32)
        .astype(jnp.bfloat16)
        .reshape(row_count, kv_local, HEAD_DIM)
    )
    keys_old = keys_cached.reshape(row_count, cache_slots, kv_local, HEAD_DIM)
    values_old = values_cached.reshape(row_count, cache_slots, kv_local, HEAD_DIM)
    visible = jnp.arange(cache_slots)[None, :] < lengths[:, None]
    scores_old = (
        jnp.einsum("rhgd,rlhd->rhgl", queries, keys_old, preferred_element_type=jnp.float32)
        * inv_root
    )
    scores_old = jnp.where(visible[:, None, None, :], scores_old, MASKED_SCORE)
    score_new = (
        jnp.einsum("rhgd,rhd->rhg", queries, key_new, preferred_element_type=jnp.float32) * inv_root
    )
    highest = jnp.maximum(jnp.max(scores_old, axis=-1), score_new)
    weight_old = jnp.exp(scores_old - highest[..., None])
    weight_new = jnp.exp(score_new - highest)
    denominator = jnp.sum(weight_old, axis=-1) + weight_new
    weight_old = (weight_old / denominator[..., None]).astype(jnp.bfloat16)
    weight_new = (weight_new / denominator).astype(jnp.bfloat16)
    attended = jnp.einsum(
        "rhgl,rlhd->rhgd", weight_old, values_old, preferred_element_type=jnp.float32
    )
    attended = (
        attended
        + weight_new.astype(jnp.float32)[..., None] * value_new.astype(jnp.float32)[:, :, None, :]
    )
    attended = attended.astype(jnp.bfloat16).reshape(row_count, kv_local * per_kv * HEAD_DIM)
    return (
        attended,
        key_new.reshape(row_count, kv_local * HEAD_DIM),
        value_new.reshape(row_count, kv_local * HEAD_DIM),
    )


def per_device(
    inputs, gains, w_query, w_key, w_value, w_out, key_cache, value_cache, cache_lens, exit_plan
):
    section_count = lax.axis_size("section")
    section_here = lax.axis_index("section")
    tensor_here = lax.axis_index("tensor")
    row_total = inputs.shape[0]
    shard_width = inputs.shape[1]
    kv_local = w_key.shape[2] // HEAD_DIM
    micro_count = 1
    block_rows = row_total // micro_count
    tick_count = section_count + micro_count - 1
    gain_row = gains[0]
    entering_all = lax.all_gather(inputs, "tensor", axis=1, tiled=True)
    carry_width = entering_all.shape[1]

    def advance(step_at, state_now):
        received, out_hidden, out_keys, out_values = state_now
        micro_at = step_at - section_here
        active = jnp.logical_and(micro_at >= 0, micro_at < micro_count)
        current = jnp.where(section_here == 0, entering_all, received)
        running = (section_here < exit_plan).astype(jnp.float32)[:, None]
        widened = current.astype(jnp.float32)
        normed = (
            widened
            * lax.rsqrt(jnp.mean(widened * widened, axis=-1, keepdims=True) + NORM_EPSILON)
            * gain_row[None, :]
        ).astype(jnp.bfloat16)
        keys_cached = key_cache[0]
        values_cached = value_cache[0]
        attended, key_new, value_new = attend(
            normed,
            cache_lens,
            w_query[0],
            w_key[0],
            w_value[0],
            keys_cached,
            values_cached,
            kv_local,
        )
        partial_value = jnp.dot(attended, w_out[0], preferred_element_type=jnp.float32)
        summed = lax.psum(partial_value, "tensor")
        following = (widened + running * summed).astype(jnp.bfloat16)
        own_piece = lax.dynamic_slice_in_dim(following, tensor_here * shard_width, shard_width, 1)
        passed = shifted(following, "section", 1)
        out_hidden = jnp.where(active, own_piece, out_hidden)
        out_keys = jnp.where(active, key_new, out_keys)
        out_values = jnp.where(active, value_new, out_values)
        return (passed, out_hidden, out_keys, out_values)

    initial = (
        jnp.zeros((block_rows, carry_width), jnp.bfloat16),
        jnp.zeros((row_total, shard_width), jnp.bfloat16),
        jnp.zeros((row_total, kv_local * HEAD_DIM), jnp.bfloat16),
        jnp.zeros((row_total, kv_local * HEAD_DIM), jnp.bfloat16),
    )
    final_state = lax.fori_loop(0, tick_count, advance, initial)
    return (final_state[1][None], final_state[2][None], final_state[3][None])


def solution(mesh):
    return jax.shard_map(
        per_device,
        mesh=mesh,
        in_specs=(
            P("group", "tensor"),
            P("section", None),
            P("section", None, "tensor"),
            P("section", None, "tensor"),
            P("section", None, "tensor"),
            P("section", "tensor", None),
            P("section", "group", None, "tensor"),
            P("section", "group", None, "tensor"),
            P("group"),
            P("group"),
        ),
        out_specs=(
            P("section", "group", "tensor"),
            P("section", "group", "tensor"),
            P("section", "group", "tensor"),
        ),
        check_vma=False,
    )
```

profile of v0, /device:TPU:24, one launch (start us, length us, event | category | flops | bytes accessed | tf_op | source)
XLA Modules:
  0.0 273.9 jit_solution(9247631473398930788)
XLA Ops:
  8.0 5.8 %all_gather.3 = bf16[24,4096]{1,0:T(8,128)(2,1)S(1)} all-gather(bf16[24,1024]{1,0:T(8,128)(2,1)} %param.12), channel_id=1, replica_groups=mesh['group'=2,'section'=4,'tensor'=4] {'tensor'}, dimensions={1}, use_global_device_ids=true | all-gather | bytes 245760 | tf_op jit(solution)/shard_map/all_gather | solution.py:106
  13.8 3.5 %squeeze.67 = bf16[24,128,2,128]{3,2,1,0:T(2,128)(2,1)} reshape(bf16[1,24,128,256]{3,2,1,0:T(8,128)(2,1)} %param.18) | data formatting | bytes 3145728 | tf_op jit(solution)/shard_map/while/body/eval_jaxpr/reshape;while/body/eval_jaxpr/squeeze | solution.py:61
  17.3 1.9 squeeze.66
  19.2 2.9 %copy.25 = bf16[1,4096,256]{1,2,0:T(8,128)(2,1)S(1)} copy(bf16[1,4096,256]{2,1,0:T(8,128)(2,1)} %param.15) | data formatting | bytes 4194304
  22.1 11.4 %copy.24 = bf16[1,4096,1024]{1,2,0:T(8,128)(2,1)} copy(bf16[1,4096,1024]{2,1,0:T(8,128)(2,1)} %param.14) | data formatting | bytes 16777216
  33.5 233.3 %while.23 = (s32[]{:T(128)}, bf16[24,4096]{1,0:T(8,128)(2,1)S(1)}, bf16[24,1024]{1,0:T(8,128)(2,1)S(1)}, bf16[24,256]{1,0:T(8,128)(2,1)S(1)}, bf16[24,256]{1,0:T...) while((s32[]{:T(128)}, bf16[24,4096]{1,0:T(8,128)(2,1)S(1)}, ...), condition=%wide.wide.region_5.6_spmd.clone, body=%wide.wide.region_0.5_spmd.clone.sunk | while | flops 518737920 | bytes 52014272 | solution.py:149
  36.0 5.8 %fusion.98 = f32[24,8,128]{2,0,1:T(8,128)S(1)} fusion(bf16[8,128,4096]{2,1,0:T(8,128)(2,1)} %bitcast.101, bf16[24,4096]{1,0:T(8,128)(2,1)S(1)} %get-tuple-element.801, f32[4096]{0:T(1024)S(1)} %bitcast.107, f32[24]{0:T(128)S(1)} %add_rsqrt_fusion.3), kind=kOutput, calls=%fused_computation.22.clone.clone.1 | convolution fusion | flops 201719808 | bytes 8700000 | tf_op jit(solution)/shard_map/while/body/eval_jaxpr/dot_general | solution.py:46
  44.5 5.3 %fusion.106 = f32[24,4096]{1,0:T(8,128)} fusion(bf16[24,1024]{1,0:T(8,128)(2,1)S(1)} %reshape.213, bf16[1,1024,4096]{2,1,0:T(8,128)(2,1)} %get-tuple-element.878), kind=kOutput, calls=%fused_computation.clone.clone.1 | convolution fusion | flops 201326592 | bytes 8830976 | tf_op jit(solution)/shard_map/while/body/eval_jaxpr/dot_general | solution.py:133
  50.0 33.7 %all-reduce.2.cloned.1.call-done = f32[24,4096]{1,0:T(8,128)} async-done(((f32[24,4096]{1,0:T(8,128)}), f32[24,4096]{1,0:T(8,128)}) %all-reduce.2.cloned.1.call-update) | async-done | bytes 393232 | tf_op jit(solution)/shard_map/while/body/eval_jaxpr/psum | solution.py:134
  84.7 1.3 collective-permute-start
  86.1 6.2 %collective-permute-done = bf16[24,4096]{1,0:T(8,128)(2,1)S(1)} collective-permute-done((bf16[24,4096]{1,0:T(8,128)(2,1)S(1)}, bf16[24,4096]{1,0:T(8,128)(2,1)S(1)}, u32[]{:S(2)}, u32[]{:S(2)}) %collective-permute-start) | collective-permute-done | bytes 196640 | tf_op jit(solution)/shard_map/while/body/eval_jaxpr/ppermute | solution.py:19
  94.7 5.8 %fusion.98 = f32[24,8,128]{2,0,1:T(8,128)S(1)} fusion(bf16[8,128,4096]{2,1,0:T(8,128)(2,1)} %bitcast.101, bf16[24,4096]{1,0:T(8,128)(2,1)S(1)} %get-tuple-element.801, f32[4096]{0:T(1024)S(1)} %bitcast.107, f32[24]{0:T(128)S(1)} %add_rsqrt_fusion.3), kind=kOutput, calls=%fused_computation.22.clone.clone.1 | convolution fusion | flops 201719808 | bytes 8700000 | tf_op jit(solution)/shard_map/while/body/eval_jaxpr/dot_general | solution.py:46
  103.2 5.3 %fusion.106 = f32[24,4096]{1,0:T(8,128)} fusion(bf16[24,1024]{1,0:T(8,128)(2,1)S(1)} %reshape.213, bf16[1,1024,4096]{2,1,0:T(8,128)(2,1)} %get-tuple-element.878), kind=kOutput, calls=%fused_computation.clone.clone.1 | convolution fusion | flops 201326592 | bytes 8830976 | tf_op jit(solution)/shard_map/while/body/eval_jaxpr/dot_general | solution.py:133
  108.7 33.1 %all-reduce.2.cloned.1.call-done = f32[24,4096]{1,0:T(8,128)} async-done(((f32[24,4096]{1,0:T(8,128)}), f32[24,4096]{1,0:T(8,128)}) %all-reduce.2.cloned.1.call-update) | async-done | bytes 393232 | tf_op jit(solution)/shard_map/while/body/eval_jaxpr/psum | solution.py:134
  142.9 1.3 collective-permute-start
  144.2 6.2 %collective-permute-done = bf16[24,4096]{1,0:T(8,128)(2,1)S(1)} collective-permute-done((bf16[24,4096]{1,0:T(8,128)(2,1)S(1)}, bf16[24,4096]{1,0:T(8,128)(2,1)S(1)}, u32[]{:S(2)}, u32[]{:S(2)}) %collective-permute-start) | collective-permute-done | bytes 196640 | tf_op jit(solution)/shard_map/while/body/eval_jaxpr/ppermute | solution.py:19
  152.8 5.8 %fusion.98 = f32[24,8,128]{2,0,1:T(8,128)S(1)} fusion(bf16[8,128,4096]{2,1,0:T(8,128)(2,1)} %bitcast.101, bf16[24,4096]{1,0:T(8,128)(2,1)S(1)} %get-tuple-element.801, f32[4096]{0:T(1024)S(1)} %bitcast.107, f32[24]{0:T(128)S(1)} %add_rsqrt_fusion.3), kind=kOutput, calls=%fused_computation.22.clone.clone.1 | convolution fusion | flops 201719808 | bytes 8700000 | tf_op jit(solution)/shard_map/while/body/eval_jaxpr/dot_general | solution.py:46
  161.4 5.3 %fusion.106 = f32[24,4096]{1,0:T(8,128)} fusion(bf16[24,1024]{1,0:T(8,128)(2,1)S(1)} %reshape.213, bf16[1,1024,4096]{2,1,0:T(8,128)(2,1)} %get-tuple-element.878), kind=kOutput, calls=%fused_computation.clone.clone.1 | convolution fusion | flops 201326592 | bytes 8830976 | tf_op jit(solution)/shard_map/while/body/eval_jaxpr/dot_general | solution.py:133
  166.8 33.1 %all-reduce.2.cloned.1.call-done = f32[24,4096]{1,0:T(8,128)} async-done(((f32[24,4096]{1,0:T(8,128)}), f32[24,4096]{1,0:T(8,128)}) %all-reduce.2.cloned.1.call-update) | async-done | bytes 393232 | tf_op jit(solution)/shard_map/while/body/eval_jaxpr/psum | solution.py:134
  202.4 6.2 %collective-permute-done = bf16[24,4096]{1,0:T(8,128)(2,1)S(1)} collective-permute-done((bf16[24,4096]{1,0:T(8,128)(2,1)S(1)}, bf16[24,4096]{1,0:T(8,128)(2,1)S(1)}, u32[]{:S(2)}, u32[]{:S(2)}) %collective-permute-start) | collective-permute-done | bytes 196640 | tf_op jit(solution)/shard_map/while/body/eval_jaxpr/ppermute | solution.py:19
  211.0 5.8 %fusion.98 = f32[24,8,128]{2,0,1:T(8,128)S(1)} fusion(bf16[8,128,4096]{2,1,0:T(8,128)(2,1)} %bitcast.101, bf16[24,4096]{1,0:T(8,128)(2,1)S(1)} %get-tuple-element.801, f32[4096]{0:T(1024)S(1)} %bitcast.107, f32[24]{0:T(128)S(1)} %add_rsqrt_fusion.3), kind=kOutput, calls=%fused_computation.22.clone.clone.1 | convolution fusion | flops 201719808 | bytes 8700000 | tf_op jit(solution)/shard_map/while/body/eval_jaxpr/dot_general | solution.py:46
  219.6 5.3 %fusion.106 = f32[24,4096]{1,0:T(8,128)} fusion(bf16[24,1024]{1,0:T(8,128)(2,1)S(1)} %reshape.213, bf16[1,1024,4096]{2,1,0:T(8,128)(2,1)} %get-tuple-element.878), kind=kOutput, calls=%fused_computation.clone.clone.1 | convolution fusion | flops 201326592 | bytes 8830976 | tf_op jit(solution)/shard_map/while/body/eval_jaxpr/dot_general | solution.py:133
  225.0 33.1 %all-reduce.2.cloned.1.call-done = f32[24,4096]{1,0:T(8,128)} async-done(((f32[24,4096]{1,0:T(8,128)}), f32[24,4096]{1,0:T(8,128)}) %all-reduce.2.cloned.1.call-update) | async-done | bytes 393232 | tf_op jit(solution)/shard_map/while/body/eval_jaxpr/psum | solution.py:134
  260.6 6.2 %collective-permute-done = bf16[24,4096]{1,0:T(8,128)(2,1)S(1)} collective-permute-done((bf16[24,4096]{1,0:T(8,128)(2,1)S(1)}, bf16[24,4096]{1,0:T(8,128)(2,1)S(1)}, u32[]{:S(2)}, u32[]{:S(2)}) %collective-permute-start) | collective-permute-done | bytes 196640 | tf_op jit(solution)/shard_map/while/body/eval_jaxpr/ppermute | solution.py:19
  (149 shorter events, 29.1 us)
Async XLA Ops:
  7.2 10.1 %copy-start.2 = (bf16[1,24,128,256]{3,2,1,0:T(8,128)(2,1)S(1)}, bf16[1,24,128,256]{3,2,1,0:T(8,128)(2,1)}, u32[]{:S(2)}) copy-start(bf16[1,24,128,256]{3,2,1,0:T(8,128)(2,1)} %param.19) | copy-start | bytes 4718596
  22.1 11.4 %copy-start.1 = (f32[1,4096]{1,0:T(1,128)S(1)}, f32[1,4096]{1,0:T(1,128)}, u32[]{:S(2)}) copy-start(f32[1,4096]{1,0:T(1,128)} %param.13) | copy-start | bytes 49156
  22.1 11.4 %copy-start.8 = (s32[24]{0:T(128)S(1)}, s32[24]{0:T(128)}, u32[]{:S(2)}) copy-start(s32[24]{0:T(128)} %param.20) | copy-start | bytes 292
  22.1 11.4 %copy-start.9 = (s32[24]{0:T(128)S(1)}, s32[24]{0:T(128)}, u32[]{:S(2)}) copy-start(s32[24]{0:T(128)} %param.21) | copy-start | bytes 292
  33.5 50.1 %all-reduce.2.cloned.1.call-start = ((), (), s32[]{:S(2)}) async-start(), calls=%async_computation | async-start | bytes 786432 | tf_op jit(solution)/shard_map/while/body/eval_jaxpr/psum | solution.py:134
  33.9 1.6 copy-start
  35.9 6.5 %copy-start.3 = (bf16[24,128,2,128]{3,2,1,0:T(2,128)(2,1)S(1)}, bf16[24,128,2,128]{3,2,1,0:T(2,128)(2,1)}, u32[]{:S(2)}) copy-start(bf16[24,128,2,128]{3,2,1,0:T(2,128)(2,1)} %get-tuple-element.881) | copy-start | bytes 4718596 | tf_op jit(solution)/shard_map/while
  41.7 2.1 copy-start.4
  84.7 7.6 %collective-permute-start = (bf16[24,4096]{1,0:T(8,128)(2,1)S(1)}, bf16[24,4096]{1,0:T(8,128)(2,1)S(1)}, u32[]{:S(2)}, u32[]{:S(2)}) collective-permute-start(bf16[24,4096]{1,0:T(8,128)(2,1)S(1)} %fusion.107), channel_id=1, source_target_pairs={{0,4},{4,8},{8,12},{1,5},{5,9},{9,13},{2,6},{6,10},{10,14},{3,7},{... | collective-permute-start | bytes 589832 | tf_op jit(solution)/shard_map/while/body/eval_jaxpr/ppermute | solution.py:19
  92.3 49.5 %all-reduce.2.cloned.1.call-start = ((), (), s32[]{:S(2)}) async-start(), calls=%async_computation | async-start | bytes 786432 | tf_op jit(solution)/shard_map/while/body/eval_jaxpr/psum | solution.py:134
  92.6 1.6 copy-start
  94.7 6.5 %copy-start.3 = (bf16[24,128,2,128]{3,2,1,0:T(2,128)(2,1)S(1)}, bf16[24,128,2,128]{3,2,1,0:T(2,128)(2,1)}, u32[]{:S(2)}) copy-start(bf16[24,128,2,128]{3,2,1,0:T(2,128)(2,1)} %get-tuple-element.881) | copy-start | bytes 4718596 | tf_op jit(solution)/shard_map/while
  100.5 2.1 copy-start.4
  142.9 7.6 %collective-permute-start = (bf16[24,4096]{1,0:T(8,128)(2,1)S(1)}, bf16[24,4096]{1,0:T(8,128)(2,1)S(1)}, u32[]{:S(2)}, u32[]{:S(2)}) collective-permute-start(bf16[24,4096]{1,0:T(8,128)(2,1)S(1)} %fusion.107), channel_id=1, source_target_pairs={{0,4},{4,8},{8,12},{1,5},{5,9},{9,13},{2,6},{6,10},{10,14},{3,7},{... | collective-permute-start | bytes 589832 | tf_op jit(solution)/shard_map/while/body/eval_jaxpr/ppermute | solution.py:19
  150.5 49.5 %all-reduce.2.cloned.1.call-start = ((), (), s32[]{:S(2)}) async-start(), calls=%async_computation | async-start | bytes 786432 | tf_op jit(solution)/shard_map/while/body/eval_jaxpr/psum | solution.py:134
  150.8 1.6 copy-start
  152.8 6.5 %copy-start.3 = (bf16[24,128,2,128]{3,2,1,0:T(2,128)(2,1)S(1)}, bf16[24,128,2,128]{3,2,1,0:T(2,128)(2,1)}, u32[]{:S(2)}) copy-start(bf16[24,128,2,128]{3,2,1,0:T(2,128)(2,1)} %get-tuple-element.881) | copy-start | bytes 4718596 | tf_op jit(solution)/shard_map/while
  158.6 2.1 copy-start.4
  201.1 7.6 %collective-permute-start = (bf16[24,4096]{1,0:T(8,128)(2,1)S(1)}, bf16[24,4096]{1,0:T(8,128)(2,1)S(1)}, u32[]{:S(2)}, u32[]{:S(2)}) collective-permute-start(bf16[24,4096]{1,0:T(8,128)(2,1)S(1)} %fusion.107), channel_id=1, source_target_pairs={{0,4},{4,8},{8,12},{1,5},{5,9},{9,13},{2,6},{6,10},{10,14},{3,7},{... | collective-permute-start | bytes 589832 | tf_op jit(solution)/shard_map/while/body/eval_jaxpr/ppermute | solution.py:19
  208.6 49.5 %all-reduce.2.cloned.1.call-start = ((), (), s32[]{:S(2)}) async-start(), calls=%async_computation | async-start | bytes 786432 | tf_op jit(solution)/shard_map/while/body/eval_jaxpr/psum | solution.py:134
  208.9 1.6 copy-start
  211.0 6.5 %copy-start.3 = (bf16[24,128,2,128]{3,2,1,0:T(2,128)(2,1)S(1)}, bf16[24,128,2,128]{3,2,1,0:T(2,128)(2,1)}, u32[]{:S(2)}) copy-start(bf16[24,128,2,128]{3,2,1,0:T(2,128)(2,1)} %get-tuple-element.881) | copy-start | bytes 4718596 | tf_op jit(solution)/shard_map/while
  216.8 2.1 copy-start.4
  259.2 7.6 %collective-permute-start = (bf16[24,4096]{1,0:T(8,128)(2,1)S(1)}, bf16[24,4096]{1,0:T(8,128)(2,1)S(1)}, u32[]{:S(2)}, u32[]{:S(2)}) collective-permute-start(bf16[24,4096]{1,0:T(8,128)(2,1)S(1)} %fusion.107), channel_id=1, source_target_pairs={{0,4},{4,8},{8,12},{1,5},{5,9},{9,13},{2,6},{6,10},{10,14},{3,7},{... | collective-permute-start | bytes 589832 | tf_op jit(solution)/shard_map/while/body/eval_jaxpr/ppermute | solution.py:19
  (3 other events, 1.9 us)
Sparse Core Ops, SparseCore 0:
  50.0 33.5 all-reduce.1
  108.7 33.0 all-reduce.1
  166.9 33.0 all-reduce.1
  225.0 33.0 all-reduce.1
where the time goes:
time: 276 us; the launch traced here: 274 us
  waiting for transfers between devices  158 us (57%)
  matrix products  56.4 us (20%)
  local copies, waits for them, and re-layouts  24.5 us (9%)
  between operations  13.8 us (5%)
  other arithmetic  9.68 us (4%)
  blocking collectives  5.8 us (2%)
  starting transfers between devices  5.22 us (2%)
    psum x4, waiting for transfers between devices, advance(): summed = lax.psum(partial_value, 'tensor')  133 us
    ppermute x4, waiting for transfers between devices, shifted(): lax.ppermute(value, axis, [(source, source + steps) for source in range(l...  24.9 us
    dot_general x4, matrix products, attend(): jnp.dot(normed, query_weight, preferred_element_type=jnp.float32)  23.1 us
    dot_general x4, matrix products, advance(): jnp.dot(attended, w_out[0], preferred_element_type=jnp.float32)  21.3 us
    unnamed x16, local copies, waits for them, and re-layouts  14.9 us
    all_gather x1, blocking collectives, per_device(): entering_all = lax.all_gather(inputs, 'tensor', axis=1, tiled=True)  5.8 us
  transfers between devices with their start and end apart: 8, of which 8 were waited for; matrix products, arithmetic and copies ran while one was open for 0% of the time, Pallas kernels for 0%

commit v1 on v0

v1 whole, which is shorter than its diff:
```python
import functools
import math

import jax
import jax.numpy as jnp
from jax import lax
from jax.experimental import pallas as pl
from jax.experimental.pallas import tpu as pltpu
from jax.sharding import PartitionSpec as P

HEAD_DIM = 128
NORM_EPSILON = 1e-05
ROPE_BASE = 500000.0
MASKED_SCORE = -1e30
MESH = pl.DeviceIdType.MESH


def relay_kernel(
    sections, tensors, groups_per_kv,
    lens_ref, plan_ref, inputs_ref, gains_ref, wq_ref, wk_ref, wv_ref, wo_ref, kc_ref, vc_ref,
    out_hidden, out_keys, out_values,
    wq, wk, wv, wo, kc, vc, gain, hid, part, arrived, piece, normed,
    pos, running, mask, queries, scores, score_new, values_new, attended,
    load_sem, hid_send, hid_recv, part_send, part_recv,
):
    rows, width = hid.shape[1], hid.shape[2]
    kv_local = wk.shape[1] // HEAD_DIM
    heads = kv_local * groups_per_kv
    slot = queries.shape[0] // rows
    slots = kc.shape[1]
    section = lax.axis_index("section")
    me = lax.axis_index("tensor")

    def load(source, target, index):
        return pltpu.make_async_copy(source, target, load_sem.at[index])

    loads = dict(
        gain=load(gains_ref, gain, 0),
        wk=load(wk_ref.at[0], wk, 1),
        wv=load(wv_ref.at[0], wv, 2),
        wq=load(wq_ref.at[0], wq, 3),
        kc=load(kc_ref.at[0], kc, 4),
        vc=load(vc_ref.at[0], vc, 5),
        wo=load(wo_ref.at[0], wo, 6),
    )
    own_entering = pltpu.make_async_copy(inputs_ref, hid.at[me], load_sem.at[7])
    for name in ("gain", "wk", "wv", "wq"):
        loads[name].start()

    @pl.when(section == 0)
    def _():
        own_entering.start()

    for name in ("kc", "vc", "wo"):
        loads[name].start()

    barrier = pltpu.get_barrier_semaphore()
    for off in range(1, tensors):
        pl.semaphore_signal(
            barrier, inc=1, device_id={"tensor": lax.rem(me + off, tensors)}, device_id_type=MESH
        )

    @pl.when(section > 0)
    def _():
        for other in range(tensors):
            pl.semaphore_signal(
                barrier, inc=1,
                device_id={"section": section - 1, "tensor": jnp.int32(other)}, device_id_type=MESH,
            )

    @pl.when(section < sections - 1)
    def _():
        for other in range(tensors):
            pl.semaphore_signal(
                barrier, inc=1,
                device_id={"section": section + 1, "tensor": jnp.int32(other)}, device_id_type=MESH,
            )

    lane = lax.broadcasted_iota(jnp.int32, (slot, slots), 1)
    for row in range(rows):
        length = lens_ref[row]
        pos[row : row + 1, :] = jnp.full((1, HEAD_DIM), length, jnp.int32).astype(jnp.float32)
        runs = jnp.full((1, HEAD_DIM), plan_ref[row], jnp.int32) > section
        running[row : row + 1, :] = runs.astype(jnp.float32)
        mask[row * slot : (row + 1) * slot, :] = (lane < length).astype(jnp.float32)
    half_lane = lax.broadcasted_iota(jnp.int32, (rows, HEAD_DIM), 1)
    half = HEAD_DIM // 2
    step_at = jnp.where(half_lane < half, half_lane, half_lane - half).astype(jnp.float32)
    frequency = jnp.exp(step_at * (-2.0 * math.log(ROPE_BASE) / HEAD_DIM))
    angles = pos[...] * frequency
    cos_part = jnp.cos(angles)
    sin_part = jnp.sin(angles)
    sin_part = jnp.where(half_lane < half, -sin_part, sin_part)

    def rotate(vectors):
        return vectors * cos_part + pltpu.roll(vectors, half, 1) * sin_part

    pl.semaphore_wait(
        barrier,
        (tensors - 1)
        + tensors * (section > 0).astype(jnp.int32)
        + tensors * (section < sections - 1).astype(jnp.int32),
    )

    def entering(off):
        return pltpu.make_async_remote_copy(
            src_ref=inputs_ref,
            dst_ref=hid.at[me],
            send_sem=hid_send.at[off],
            recv_sem=hid_recv.at[me],
            device_id={"tensor": lax.rem(me + off, tensors)},
            device_id_type=MESH,
        )

    def await_hidden(source):
        pltpu.make_async_remote_copy(
            src_ref=hid.at[source],
            dst_ref=hid.at[source],
            send_sem=hid_send.at[0],
            recv_sem=hid_recv.at[source],
            device_id={"tensor": lax.rem(me + 1, tensors)},
            device_id_type=MESH,
        ).wait_recv()

    @pl.when(section == 0)
    def _():
        for off in range(1, tensors):
            entering(off).start()
        own_entering.wait()
        for off in range(1, tensors):
            await_hidden(lax.rem(me + off, tensors))
        for off in range(1, tensors):
            entering(off).wait_send()

    @pl.when(section > 0)
    def _():
        for source in range(tensors):
            await_hidden(source)

    loads["gain"].wait()
    squares = jnp.zeros((rows, 1), jnp.float32)
    for source in range(tensors):
        wide = hid[source].astype(jnp.float32)
        squares = squares + jnp.sum(wide * wide, axis=-1, keepdims=True)
    scale = lax.rsqrt(squares / (tensors * width) + NORM_EPSILON)
    for source in range(tensors):
        at = slice(source * width, (source + 1) * width)
        normed[:, at] = (hid[source].astype(jnp.float32) * scale * gain[:, at]).astype(jnp.bfloat16)

    entered = normed[...]
    loads["wk"].wait()
    key_new = jnp.dot(entered, wk[...], preferred_element_type=jnp.float32)
    loads["wv"].wait()
    value_new = jnp.dot(entered, wv[...], preferred_element_type=jnp.float32).astype(jnp.bfloat16)
    out_values[0] = value_new
    keys = []
    values = []
    for kv in range(kv_local):
        at = slice(kv * HEAD_DIM, (kv + 1) * HEAD_DIM)
        rotated = rotate(key_new[:, at]).astype(jnp.bfloat16)
        out_keys[0, :, at] = rotated
        keys.append(rotated.astype(jnp.float32))
        values.append(value_new[:, at].astype(jnp.float32))

    loads["wq"].wait()
    inv_root = 1.0 / math.sqrt(HEAD_DIM)
    if heads < slot:
        queries[...] = jnp.zeros_like(queries)
        score_new[...] = jnp.zeros_like(score_new)
        values_new[...] = jnp.zeros_like(values_new)
    tile = min(256, heads * HEAD_DIM)
    for start in range(0, heads * HEAD_DIM, tile):
        product = jnp.dot(
            entered, wq[:, start : start + tile], preferred_element_type=jnp.float32
        )
        for inner in range(tile // HEAD_DIM):
            head = start // HEAD_DIM + inner
            kv = head // groups_per_kv
            query = rotate(product[:, inner * HEAD_DIM : (inner + 1) * HEAD_DIM])
            query = query.astype(jnp.bfloat16).astype(jnp.float32)
            at = pl.ds(head, rows, stride=slot)
            queries[at, :] = query
            score = jnp.sum(query * keys[kv], axis=-1, keepdims=True) * inv_root
            score_new[at, :] = jnp.broadcast_to(score, (rows, HEAD_DIM))
            values_new[at, :] = values[kv]

    loads["kc"].wait()
    head_of = lax.broadcasted_iota(jnp.int32, (slot, HEAD_DIM), 0) // groups_per_kv
    for row in range(rows):
        at = slice(row * slot, (row + 1) * slot)
        query = queries[at, :]
        spread = jnp.concatenate(
            [jnp.where(head_of == kv, query, 0.0) for kv in range(kv_local)], axis=1
        ).astype(jnp.bfloat16)
        scores[at, :] = lax.dot_general(
            spread, kc[row], (((1,), (1,)), ((), ())), preferred_element_type=jnp.float32
        )

    old = jnp.where(mask[...] > 0.0, scores[...] * inv_root, MASKED_SCORE)
    new = score_new[:, :1]
    highest = jnp.maximum(jnp.max(old, axis=-1, keepdims=True), new)
    weight_old = jnp.exp(old - highest)
    weight_new = jnp.exp(new - highest)
    denominator = jnp.sum(weight_old, axis=-1, keepdims=True) + weight_new
    scores[...] = weight_old / denominator
    weight_new = (weight_new / denominator).astype(jnp.bfloat16).astype(jnp.float32)
    values_new[...] = values_new[...] * weight_new

    loads["vc"].wait()
    for row in range(rows):
        at = slice(row * slot, (row + 1) * slot)
        mixed = jnp.dot(
            scores[at, :].astype(jnp.bfloat16), vc[row], preferred_element_type=jnp.float32
        )
        taken = mixed[:, :HEAD_DIM]
        for kv in range(1, kv_local):
            taken = jnp.where(head_of == kv, mixed[:, kv * HEAD_DIM : (kv + 1) * HEAD_DIM], taken)
        attended[at, :] = taken + values_new[at, :]

    flat = jnp.concatenate(
        [
            attended[pl.ds(head, rows, stride=slot), :].astype(jnp.bfloat16)
            for head in range(heads)
        ],
        axis=1,
    )

    loads["wo"].wait()

    def send_part(off):
        peer = lax.rem(me + off, tensors)
        return pltpu.make_async_remote_copy(
            src_ref=part.at[off],
            dst_ref=arrived.at[off],
            send_sem=part_send.at[off],
            recv_sem=part_recv.at[off],
            device_id={"tensor": peer},
            device_id_type=MESH,
        )

    def project(target):
        columns = pl.ds(pl.multiple_of(target * width, width), width)
        return jnp.dot(flat, wo[:, columns], preferred_element_type=jnp.float32)

    order = sorted(range(1, tensors), key=lambda off: -min(off, tensors - off))
    for off in order:
        part[off] = project(lax.rem(me + off, tensors)).astype(jnp.bfloat16)
        send_part(off).start()
    total = project(me)
    for off in range(1, tensors):
        send_part(off).wait_recv()
        total = total + arrived[off].astype(jnp.float32)
    following = (hid[me].astype(jnp.float32) + running[:, :1] * total).astype(jnp.bfloat16)
    piece[...] = following

    def pass_on(other):
        return pltpu.make_async_remote_copy(
            src_ref=piece,
            dst_ref=hid.at[me],
            send_sem=hid_send.at[other],
            recv_sem=hid_recv.at[me],
            device_id={"section": section + 1, "tensor": lax.rem(me + other, tensors)},
            device_id_type=MESH,
        )

    @pl.when(section < sections - 1)
    def _():
        for other in range(tensors):
            pass_on(other).start()

    out_hidden[0] = following
    for off in range(1, tensors):
        send_part(off).wait_send()

    @pl.when(section < sections - 1)
    def _():
        for other in range(tensors):
            pass_on(other).wait_send()


def solution(mesh):
    sections = mesh.shape["section"]
    tensors = mesh.shape["tensor"]

    def per_device(
        inputs, gains, w_query, w_key, w_value, w_out, key_cache, value_cache, cache_lens, exit_plan
    ):
        rows, width = inputs.shape
        features = gains.shape[1]
        query_width = w_query.shape[2]
        kv_width = w_key.shape[2]
        heads = query_width // HEAD_DIM
        groups_per_kv = query_width // kv_width
        slot = -(-heads // 8) * 8
        slots = key_cache.shape[2]
        any_spec = pl.BlockSpec(memory_space=pl.ANY)
        smem_spec = pl.BlockSpec(memory_space=pltpu.SMEM)
        vmem_spec = pl.BlockSpec(memory_space=pltpu.VMEM)
        bf16, f32 = jnp.bfloat16, jnp.float32
        return pl.pallas_call(
            functools.partial(relay_kernel, sections, tensors, groups_per_kv),
            out_shape=(
                jax.ShapeDtypeStruct((1, rows, width), bf16),
                jax.ShapeDtypeStruct((1, rows, kv_width), bf16),
                jax.ShapeDtypeStruct((1, rows, kv_width), bf16),
            ),
            in_specs=[smem_spec] * 2 + [any_spec] * 8,
            out_specs=(vmem_spec,) * 3,
            scratch_shapes=[
                pltpu.VMEM((features, query_width), bf16),
                pltpu.VMEM((features, kv_width), bf16),
                pltpu.VMEM((features, kv_width), bf16),
                pltpu.VMEM((query_width, features), bf16),
                pltpu.VMEM((rows, slots, kv_width), bf16),
                pltpu.VMEM((rows, slots, kv_width), bf16),
                pltpu.VMEM((1, features), f32),
                pltpu.VMEM((tensors, rows, width), bf16),
                pltpu.VMEM((tensors, rows, width), bf16),
                pltpu.VMEM((tensors, rows, width), bf16),
                pltpu.VMEM((rows, width), bf16),
                pltpu.VMEM((rows, features), bf16),
                pltpu.VMEM((rows, HEAD_DIM), f32),
                pltpu.VMEM((rows, HEAD_DIM), f32),
                pltpu.VMEM((rows * slot, slots), f32),
                pltpu.VMEM((rows * slot, HEAD_DIM), f32),
                pltpu.VMEM((rows * slot, slots), f32),
                pltpu.VMEM((rows * slot, HEAD_DIM), f32),
                pltpu.VMEM((rows * slot, HEAD_DIM), f32),
                pltpu.VMEM((rows * slot, HEAD_DIM), f32),
                pltpu.SemaphoreType.DMA((8,)),
                pltpu.SemaphoreType.DMA((tensors,)),
                pltpu.SemaphoreType.DMA((tensors,)),
                pltpu.SemaphoreType.DMA((tensors,)),
                pltpu.SemaphoreType.DMA((tensors,)),
            ],
            compiler_params=pltpu.CompilerParams(
                collective_id=0, has_side_effects=True, vmem_limit_bytes=48 * 1024 * 1024
            ),
            name="relay",
        )(
            cache_lens, exit_plan, inputs, gains, w_query, w_key, w_value, w_out,
            key_cache, value_cache,
        )

    return jax.shard_map(
        per_device,
        mesh=mesh,
        in_specs=(
            P("group", "tensor"),
            P("section", None),
            P("section", None, "tensor"),
            P("section", None, "tensor"),
            P("section", None, "tensor"),
            P("section", "tensor", None),
            P("section", "group", None, "tensor"),
            P("section", "group", None, "tensor"),
            P("group"),
            P("group"),
        ),
        out_specs=(
            P("section", "group", "tensor"),
            P("section", "group", "tensor"),
            P("section", "group", "tensor"),
        ),
        check_vma=False,
    )
```

time: 276 us -> 70.1 us (0.25)
  waiting for transfers between devices: 158 us -> 0 us
  Pallas kernels: 0 us -> 60.1 us
  matrix products: 56.4 us -> 0 us
  local copies, waits for them, and re-layouts: 24.5 us -> 9.04 us
  between operations: 13.8 us -> 0.66 us
  other arithmetic: 9.68 us -> 0 us
  blocking collectives: 5.8 us -> 0 us
  starting transfers between devices: 5.22 us -> 0 us
    psum x4 -> x0, waiting for transfers between devices: 133 us -> none  [advance(): summed = lax.psum(partial_value, 'tensor')]
    pallas_call x0 -> x1, Pallas kernels: none -> 60.1 us  [per_device(): pl.pallas_call(functools.partial(relay_kernel, sections, tensors, groups_...]
    dot_general x28 -> x0, matrix products: 56.4 us -> none  [the longest x4 23.1 us: attend(): jnp.dot(normed, query_weight, preferred_element_type=jnp.float32)]
    ppermute x4 -> x0, waiting for transfers between devices: 24.9 us -> none  [shifted(): lax.ppermute(value, axis, [(source, source + steps) for source in range(l...]
    unnamed x16 -> x17, local copies, waits for them, and re-layouts: 14.9 us -> 9.04 us
    all_gather x1 -> x0, blocking collectives: 5.8 us -> none  [per_device(): entering_all = lax.all_gather(inputs, 'tensor', axis=1, tiled=True)]
    convert_element_type x13 -> x0, other arithmetic: 5.55 us -> none  [the longest x4 4.44 us: advance(): following = (widened + running * summed).astype(jnp.bfloat16)]
    squeeze x2 -> x0, local copies, waits for them, and re-layouts: 5.39 us -> none  [the longest x1 3.5 us: attend(): keys_old = keys_cached.reshape(row_count, cache_slots, kv_local, HEAD_DIM)]
  transfers between devices with their start and end apart: 8 -> 0, of which waited for: 8 -> 0; matrix products, arithmetic and copies ran while one was open for 0% -> 0% of each run, Pallas kernels for 0% -> 0%
where the time goes in v1:
time: 70.1 us; the launch traced here: 69.8 us
  Pallas kernels  60.1 us (86%)
  local copies, waits for them, and re-layouts  9.04 us (13%)
    pallas_call x1, Pallas kernels, per_device(): pl.pallas_call(functools.partial(relay_kernel, sections, tensors, groups_...  60.1 us
    unnamed x17, local copies, waits for them, and re-layouts  9.04 us

profile of v1, /device:TPU:24, one launch (start us, length us, event | category | flops | bytes accessed | tf_op | source)
XLA Modules:
  0.0 69.8 jit_solution(10173821264592577338)
XLA Ops:
  0.6 0.0 copy-start
  0.6 1.6 %copy-done = bf16[1,4096,256]{2,1,0:T(8,128)(2,1)S(1)} copy-done((bf16[1,4096,256]{2,1,0:T(8,128)(2,1)S(1)}, bf16[1,4096,256]{2,1,0:T(8,128)(2,1)}, u32[]{:S(2)}) %copy-start) | copy-done | bytes 2097176
  2.2 0.0 copy-start.1
  2.2 1.4 %copy-done.1 = bf16[1,24,128,256]{3,2,1,0:T(8,128)(2,1)S(1)} copy-done((bf16[1,24,128,256]{3,2,1,0:T(8,128)(2,1)S(1)}, bf16[1,24,128,256]{3,2,1,0:T(8,128)(2,1)}, u32[]{:S(2)}) %copy-start.1) | copy-done | bytes 1572888
  3.6 0.0 copy-start.2
  3.6 1.4 %copy-done.2 = bf16[1,24,128,256]{3,2,1,0:T(8,128)(2,1)S(1)} copy-done((bf16[1,24,128,256]{3,2,1,0:T(8,128)(2,1)S(1)}, bf16[1,24,128,256]{3,2,1,0:T(8,128)(2,1)}, u32[]{:S(2)}) %copy-start.2) | copy-done | bytes 1572888
  5.0 0.0 copy-start.3
  5.0 0.8 %copy-done.3 = bf16[24,1024]{1,0:T(8,128)(2,1)S(1)} copy-done((bf16[24,1024]{1,0:T(8,128)(2,1)S(1)}, bf16[24,1024]{1,0:T(8,128)(2,1)}, u32[]{:S(2)}) %copy-start.3) | copy-done | bytes 49176
  5.8 0.0 copy-start.4
  5.8 0.7 %copy-done.4 = f32[1,4096]{1,0:T(1,128)S(1)} copy-done((f32[1,4096]{1,0:T(1,128)S(1)}, f32[1,4096]{1,0:T(1,128)}, u32[]{:S(2)}) %copy-start.4) | copy-done | bytes 16408
  6.6 0.0 copy-start.5
  6.6 0.7 copy-done.5
  7.2 0.0 copy-start.6
  7.2 0.7 copy-done.6
  7.9 60.1 %relay.1 = (bf16[1,24,1024]{2,1,0:T(8,128)(2,1)S(1)}, bf16[1,24,256]{2,1,0:T(8,128)(2,1)S(1)}, bf16[1,24,256]{2,1,0:T(8,128)(2,1)S(1)}) custom-call(s32[24]{0:T(128)S(1)} %copy-done.5, s32[24]{0:T(128)S(1)} %copy-done.6, bf16[24,1024]{1,0:T(8,128)(2,1)S(1)} %copy-done.3, f32[1,4096]{1,0:T(1,128)S(1)} %copy-done.4, bf16[1,4096,1024]{2,1,0:T(8,128)(2,1)} %wq_ref.1, ...), custom_call_target="tpu_custom_call" | custom-call | tf_op jit(solution)/shard_map/relay/pallas_call | solution.py:300
  68.0 0.6 copy.16
  68.6 0.6 copy.17
  69.2 0.6 copy.18
Async XLA Ops:
  0.6 1.6 %copy-start = (bf16[1,4096,256]{2,1,0:T(8,128)(2,1)S(1)}, bf16[1,4096,256]{2,1,0:T(8,128)(2,1)}, u32[]{:S(2)}) copy-start(bf16[1,4096,256]{2,1,0:T(8,128)(2,1)} %wk_ref.1) | copy-start | bytes 6291460
  2.2 1.4 %copy-start.1 = (bf16[1,24,128,256]{3,2,1,0:T(8,128)(2,1)S(1)}, bf16[1,24,128,256]{3,2,1,0:T(8,128)(2,1)}, u32[]{:S(2)}) copy-start(bf16[1,24,128,256]{3,2,1,0:T(8,128)(2,1)} %kc_ref.1) | copy-start | bytes 4718596
  3.6 1.4 %copy-start.2 = (bf16[1,24,128,256]{3,2,1,0:T(8,128)(2,1)S(1)}, bf16[1,24,128,256]{3,2,1,0:T(8,128)(2,1)}, u32[]{:S(2)}) copy-start(bf16[1,24,128,256]{3,2,1,0:T(8,128)(2,1)} %vc_ref.1) | copy-start | bytes 4718596
  5.0 0.8 %copy-start.3 = (bf16[24,1024]{1,0:T(8,128)(2,1)S(1)}, bf16[24,1024]{1,0:T(8,128)(2,1)}, u32[]{:S(2)}) copy-start(bf16[24,1024]{1,0:T(8,128)(2,1)} %inputs_ref.1) | copy-start | bytes 147460
  5.8 0.7 %copy-start.4 = (f32[1,4096]{1,0:T(1,128)S(1)}, f32[1,4096]{1,0:T(1,128)}, u32[]{:S(2)}) copy-start(f32[1,4096]{1,0:T(1,128)} %gains_ref.1) | copy-start | bytes 49156
  6.6 0.7 copy-start.5
  7.2 0.7 copy-start.6

commit v2 on v1

--- a/solution.py
+++ b/solution.py
@@ -19,20 +19,31 @@
     sections, tensors, groups_per_kv,
     lens_ref, plan_ref, inputs_ref, gains_ref, wq_ref, wk_ref, wv_ref, wo_ref, kc_ref, vc_ref,
     out_hidden, out_keys, out_values,
-    wq, wk, wv, wo, kc, vc, gain, hid, part, arrived, piece, normed,
+    wq, wk, wv, wo, kc, vc, gain, hid, before, part, part_in, chip_sum, sums_in, piece_in, normed,
     pos, running, mask, queries, scores, score_new, values_new, attended,
-    load_sem, hid_send, hid_recv, part_send, part_recv,
+    load_sem, enter_send, enter_recv, half_send, half_recv, before_send, before_recv,
+    part_send, part_recv, sums_send, sums_recv, piece_send, piece_recv,
 ):
-    rows, width = hid.shape[1], hid.shape[2]
+    rows, width = hid.shape[2], hid.shape[3]
+    chips = tensors // 2
     kv_local = wk.shape[1] // HEAD_DIM
     heads = kv_local * groups_per_kv
     slot = queries.shape[0] // rows
     slots = kc.shape[1]
     section = lax.axis_index("section")
     me = lax.axis_index("tensor")
+    chip = me // 2
+    core = lax.rem(me, 2)
+    sibling = {"tensor": 2 * chip + 1 - core}
 
     def load(source, target, index):
         return pltpu.make_async_copy(source, target, load_sem.at[index])
+
+    def remote(source, target, send_sem, recv_sem, device):
+        return pltpu.make_async_remote_copy(
+            src_ref=source, dst_ref=target, send_sem=send_sem, recv_sem=recv_sem,
+            device_id=device, device_id_type=MESH,
+        )
 
     loads = dict(
         gain=load(gains_ref, gain, 0),
@@ -43,45 +54,45 @@
         vc=load(vc_ref.at[0], vc, 5),
         wo=load(wo_ref.at[0], wo, 6),
     )
-    own_entering = pltpu.make_async_copy(inputs_ref, hid.at[me], load_sem.at[7])
-    for name in ("gain", "wk", "wv", "wq"):
+    own_entering = pltpu.make_async_copy(inputs_ref, hid.at[core, chip], load_sem.at[7])
+
+    @pl.when(section == 0)
+    def _():
+        own_entering.start()
+
+    for name in ("gain", "wk", "wv", "wq", "kc"):
         loads[name].start()
 
-    @pl.when(section == 0)
-    def _():
-        own_entering.start()
-
-    for name in ("kc", "vc", "wo"):
-        loads[name].start()
+    @pl.when(section > 0)
+    def _():
+        for name in ("vc", "wo"):
+            loads[name].start()
 
     barrier = pltpu.get_barrier_semaphore()
+
+    def greet(device):
+        pl.semaphore_signal(barrier, inc=1, device_id=device, device_id_type=MESH)
+
     for off in range(1, tensors):
-        pl.semaphore_signal(
-            barrier, inc=1, device_id={"tensor": lax.rem(me + off, tensors)}, device_id_type=MESH
-        )
+        greet({"tensor": lax.rem(me + off, tensors)})
 
     @pl.when(section > 0)
     def _():
-        for other in range(tensors):
-            pl.semaphore_signal(
-                barrier, inc=1,
-                device_id={"section": section - 1, "tensor": jnp.int32(other)}, device_id_type=MESH,
-            )
+        for other in range(chips):
+            greet({"section": section - 1, "tensor": 2 * other + core})
 
     @pl.when(section < sections - 1)
     def _():
-        for other in range(tensors):
-            pl.semaphore_signal(
-                barrier, inc=1,
-                device_id={"section": section + 1, "tensor": jnp.int32(other)}, device_id_type=MESH,
-            )
+        for other in range(chips):
+            greet({"section": section + 1, "tensor": 2 * other + core})
 
     lane = lax.broadcasted_iota(jnp.int32, (slot, slots), 1)
     for row in range(rows):
         length = lens_ref[row]
         pos[row : row + 1, :] = jnp.full((1, HEAD_DIM), length, jnp.int32).astype(jnp.float32)
-        runs = jnp.full((1, HEAD_DIM), plan_ref[row], jnp.int32) > section
-        running[row : row + 1, :] = runs.astype(jnp.float32)
+        planned = jnp.full((1, HEAD_DIM), plan_ref[row], jnp.int32)
+        running[0, row : row + 1, :] = (planned > section).astype(jnp.float32)
+        running[1, row : row + 1, :] = (planned > section - 1).astype(jnp.float32)
         mask[row * slot : (row + 1) * slot, :] = (lane < length).astype(jnp.float32)
     half_lane = lax.broadcasted_iota(jnp.int32, (rows, HEAD_DIM), 1)
     half = HEAD_DIM // 2
@@ -98,29 +109,31 @@
     pl.semaphore_wait(
         barrier,
         (tensors - 1)
-        + tensors * (section > 0).astype(jnp.int32)
-        + tensors * (section < sections - 1).astype(jnp.int32),
+        + chips * (section > 0).astype(jnp.int32)
+        + chips * (section < sections - 1).astype(jnp.int32),
     )
 
     def entering(off):
-        return pltpu.make_async_remote_copy(
-            src_ref=inputs_ref,
-            dst_ref=hid.at[me],
-            send_sem=hid_send.at[off],
-            recv_sem=hid_recv.at[me],
-            device_id={"tensor": lax.rem(me + off, tensors)},
-            device_id_type=MESH,
-        )
-
-    def await_hidden(source):
-        pltpu.make_async_remote_copy(
-            src_ref=hid.at[source],
-            dst_ref=hid.at[source],
-            send_sem=hid_send.at[0],
-            recv_sem=hid_recv.at[source],
-            device_id={"tensor": lax.rem(me + 1, tensors)},
-            device_id_type=MESH,
-        ).wait_recv()
+        return remote(
+            inputs_ref, hid.at[core, chip], enter_send.at[off], enter_recv.at[core, chip],
+            {"tensor": lax.rem(me + off, tensors)},
+        )
+
+    def swap_half(half, at):
+        return remote(
+            hid.at[half, at], hid.at[half, at], half_send.at[at], half_recv.at[at], sibling
+        )
+
+    def send_sum(target, at):
+        return remote(
+            chip_sum.at[at], sums_in.at[chip, at], sums_send.at[target, at],
+            sums_recv.at[chip, at], {"section": section + 1, "tensor": 2 * target + core},
+        )
+
+    def send_before():
+        return remote(
+            hid.at[core], before, before_send.at[0], before_recv.at[0], {"section": section + 1}
+        )
 
     @pl.when(section == 0)
     def _():
@@ -128,24 +141,49 @@
             entering(off).start()
         own_entering.wait()
         for off in range(1, tensors):
-            await_hidden(lax.rem(me + off, tensors))
+            other = lax.rem(me + off, tensors)
+            at = (lax.rem(other, 2), other // 2)
+            remote(
+                hid.at[at], hid.at[at], enter_send.at[off], enter_recv.at[at], sibling
+            ).wait_recv()
+        for name in ("vc", "wo"):
+            loads[name].start()
         for off in range(1, tensors):
             entering(off).wait_send()
 
     @pl.when(section > 0)
     def _():
-        for source in range(tensors):
-            await_hidden(source)
+        remote(
+            before, before, before_send.at[0], before_recv.at[0], {"section": section - 1}
+        ).wait_recv()
+        for at in range(chips):
+            total = jnp.zeros((rows, width), jnp.float32)
+            for source in range(chips):
+                remote(
+                    sums_in.at[source, at], sums_in.at[source, at], sums_send.at[source, at],
+                    sums_recv.at[source, at], {"section": section - 1},
+                ).wait_recv()
+                total = total + sums_in[source, at].astype(jnp.float32)
+            wide = before[at].astype(jnp.float32)
+            hid[core, at] = (wide + running[1, :, :1] * total).astype(jnp.bfloat16)
+            swap_half(core, at).start()
+        for at in range(chips):
+            swap_half(1 - core, at).wait_recv()
+
+    @pl.when(section < sections - 1)
+    def _():
+        send_before().start()
 
     loads["gain"].wait()
     squares = jnp.zeros((rows, 1), jnp.float32)
     for source in range(tensors):
-        wide = hid[source].astype(jnp.float32)
+        wide = hid[source % 2, source // 2].astype(jnp.float32)
         squares = squares + jnp.sum(wide * wide, axis=-1, keepdims=True)
     scale = lax.rsqrt(squares / (tensors * width) + NORM_EPSILON)
     for source in range(tensors):
         at = slice(source * width, (source + 1) * width)
-        normed[:, at] = (hid[source].astype(jnp.float32) * scale * gain[:, at]).astype(jnp.bfloat16)
+        wide = hid[source % 2, source // 2].astype(jnp.float32)
+        normed[:, at] = (wide * scale * gain[:, at]).astype(jnp.bfloat16)
 
     entered = normed[...]
     loads["wk"].wait()
@@ -227,60 +265,77 @@
 
     loads["wo"].wait()
 
-    def send_part(off):
-        peer = lax.rem(me + off, tensors)
-        return pltpu.make_async_remote_copy(
-            src_ref=part.at[off],
-            dst_ref=arrived.at[off],
-            send_sem=part_send.at[off],
-            recv_sem=part_recv.at[off],
-            device_id={"tensor": peer},
-            device_id_type=MESH,
-        )
-
-    def project(target):
-        columns = pl.ds(pl.multiple_of(target * width, width), width)
+    def project(half, at):
+        start = (2 * at + half) * width
+        columns = pl.ds(pl.multiple_of(start, width), width)
         return jnp.dot(flat, wo[:, columns], preferred_element_type=jnp.float32)
 
-    order = sorted(range(1, tensors), key=lambda off: -min(off, tensors - off))
-    for off in order:
-        part[off] = project(lax.rem(me + off, tensors)).astype(jnp.bfloat16)
-        send_part(off).start()
-    total = project(me)
-    for off in range(1, tensors):
-        send_part(off).wait_recv()
-        total = total + arrived[off].astype(jnp.float32)
-    following = (hid[me].astype(jnp.float32) + running[:, :1] * total).astype(jnp.bfloat16)
-    piece[...] = following
-
-    def pass_on(other):
-        return pltpu.make_async_remote_copy(
-            src_ref=piece,
-            dst_ref=hid.at[me],
-            send_sem=hid_send.at[other],
-            recv_sem=hid_recv.at[me],
-            device_id={"section": section + 1, "tensor": lax.rem(me + other, tensors)},
-            device_id_type=MESH,
-        )
+    def send_part(at):
+        return remote(
+            part.at[at], part_in.at[at], part_send.at[at], part_recv.at[at], sibling
+        )
+
+    def send_piece(at):
+        return remote(
+            chip_sum.at[at], piece_in.at[chip], piece_send.at[at], piece_recv.at[chip],
+            {"tensor": 2 * at + core},
+        )
+
+    for at in range(chips):
+        part[at] = project(1 - core, at).astype(jnp.bfloat16)
+        send_part(at).start()
+    for at in range(chips):
+        own = project(core, at)
+        send_part(at).wait_recv()
+        chip_sum[at] = (own + part_in[at].astype(jnp.float32)).astype(jnp.bfloat16)
+
+        @pl.when(section < sections - 1)
+        def _():
+            for target in range(chips):
+                send_sum(target, at).start()
+
+        @pl.when(chip != at)
+        def _():
+            send_piece(at).start()
+
+    piece_in[chip] = chip_sum[chip]
+    total = jnp.zeros((rows, width), jnp.float32)
+    for source in range(chips):
+        @pl.when(chip != source)
+        def _():
+            remote(
+                piece_in.at[source], piece_in.at[source], piece_send.at[source],
+                piece_recv.at[source], sibling,
+            ).wait_recv()
+
+        total = total + piece_in[source].astype(jnp.float32)
+    wide = hid[core, chip].astype(jnp.float32)
+    out_hidden[0] = (wide + running[0, :, :1] * total).astype(jnp.bfloat16)
+
+    @pl.when(section > 0)
+    def _():
+        for at in range(chips):
+            swap_half(core, at).wait_send()
 
     @pl.when(section < sections - 1)
     def _():
-        for other in range(tensors):
-            pass_on(other).start()
-
-    out_hidden[0] = following
-    for off in range(1, tensors):
-        send_part(off).wait_send()
-
-    @pl.when(section < sections - 1)
-    def _():
-        for other in range(tensors):
-            pass_on(other).wait_send()
+        send_before().wait_send()
+        for at in range(chips):
+            for target in range(chips):
+                send_sum(target, at).wait_send()
+
+    for at in range(chips):
+        send_part(at).wait_send()
+
+        @pl.when(chip != at)
+        def _():
+            send_piece(at).wait_send()
 
 
 def solution(mesh):
     sections = mesh.shape["section"]
     tensors = mesh.shape["tensor"]
+    chips = tensors // 2
 
     def per_device(
         inputs, gains, w_query, w_key, w_value, w_out, key_cache, value_cache, cache_lens, exit_plan
@@ -314,13 +369,16 @@
                 pltpu.VMEM((rows, slots, kv_width), bf16),
                 pltpu.VMEM((rows, slots, kv_width), bf16),
                 pltpu.VMEM((1, features), f32),
-                pltpu.VMEM((tensors, rows, width), bf16),
-                pltpu.VMEM((tensors, rows, width), bf16),
-                pltpu.VMEM((tensors, rows, width), bf16),
-                pltpu.VMEM((rows, width), bf16),
+                pltpu.VMEM((2, chips, rows, width), bf16),
+                pltpu.VMEM((chips, rows, width), bf16),
+                pltpu.VMEM((chips, rows, width), bf16),
+                pltpu.VMEM((chips, rows, width), bf16),
+                pltpu.VMEM((chips, rows, width), bf16),
+                pltpu.VMEM((chips, chips, rows, width), bf16),
+                pltpu.VMEM((chips, rows, width), bf16),
                 pltpu.VMEM((rows, features), bf16),
                 pltpu.VMEM((rows, HEAD_DIM), f32),
-                pltpu.VMEM((rows, HEAD_DIM), f32),
+                pltpu.VMEM((2, rows, HEAD_DIM), f32),
                 pltpu.VMEM((rows * slot, slots), f32),
                 pltpu.VMEM((rows * slot, HEAD_DIM), f32),
                 pltpu.VMEM((rows * slot, slots), f32),
@@ -329,12 +387,20 @@
                 pltpu.VMEM((rows * slot, HEAD_DIM), f32),
                 pltpu.SemaphoreType.DMA((8,)),
                 pltpu.SemaphoreType.DMA((tensors,)),
-                pltpu.SemaphoreType.DMA((tensors,)),
-                pltpu.SemaphoreType.DMA((tensors,)),
-                pltpu.SemaphoreType.DMA((tensors,)),
+                pltpu.SemaphoreType.DMA((2, chips)),
+                pltpu.SemaphoreType.DMA((chips,)),
+                pltpu.SemaphoreType.DMA((chips,)),
+                pltpu.SemaphoreType.DMA((1,)),
+                pltpu.SemaphoreType.DMA((1,)),
+                pltpu.SemaphoreType.DMA((chips,)),
+                pltpu.SemaphoreType.DMA((chips,)),
+                pltpu.SemaphoreType.DMA((chips, chips)),
+                pltpu.SemaphoreType.DMA((chips, chips)),
+                pltpu.SemaphoreType.DMA((chips,)),
+                pltpu.SemaphoreType.DMA((chips,)),
             ],
             compiler_params=pltpu.CompilerParams(
-                collective_id=0, has_side_effects=True, vmem_limit_bytes=48 * 1024 * 1024
+                collective_id=0, has_side_effects=True, vmem_limit_bytes=63 * 1024 * 1024
             ),
             name="relay",
         )(

time: 70.1 us -> 60.8 us (0.87)
  local copies, waits for them, and re-layouts: 9.04 us -> 4.03 us
  Pallas kernels: 60.1 us -> 55.8 us
    unnamed x17 -> x3, local copies, waits for them, and re-layouts: 9.04 us -> 4.03 us
    pallas_call x1, Pallas kernels: 60.1 us -> 55.8 us  [per_device(): pl.pallas_call(functools.partial(relay_kernel, sections, tensors, groups_...]
where the time goes in v2:
time: 60.8 us; the launch traced here: 60.5 us
  Pallas kernels  55.8 us (92%)
  local copies, waits for them, and re-layouts  4.03 us (7%)
  between operations  0.64 us (1%)
    pallas_call x1, Pallas kernels, per_device(): pl.pallas_call(functools.partial(relay_kernel, sections, tensors, groups_...  55.8 us
    unnamed x3, local copies, waits for them, and re-layouts  4.03 us

profile of v2, /device:TPU:24, one launch (start us, length us, event | category | flops | bytes accessed | tf_op | source)
XLA Modules:
  0.0 60.5 jit_solution(11522334723590887796)
XLA Ops:
  0.6 55.8 %relay.1 = (bf16[1,24,1024]{2,1,0:T(8,128)(2,1)}, bf16[1,24,256]{2,1,0:T(8,128)(2,1)}, bf16[1,24,256]{2,1,0:T(8,128)(2,1)}) custom-call(s32[24]{0:T(128)} %lens_ref.1, s32[24]{0:T(128)} %plan_ref.1, bf16[24,1024]{1,0:T(8,128)(2,1)} %inputs_ref.1, f32[1,4096]{1,0:T(1,128)} %gains_ref.1, bf16[1,4096,1024]{2,1,0:T(8,128)(2,1)} %wq_ref.1, ...), custom_call_target="tpu_custom_call" | custom-call | tf_op jit(solution)/shard_map/relay/pallas_call | solution.py:355
  56.5 1.4 %copy.16 = bf16[1,24,1024]{2,1,0:T(8,128)(2,1)} copy(bf16[1,24,1024]{2,1,0:T(8,128)(2,1)} %get-tuple-element.6) | data formatting | bytes 98304
  57.9 1.3 %copy.17 = bf16[1,24,256]{2,1,0:T(8,128)(2,1)} copy(bf16[1,24,256]{2,1,0:T(8,128)(2,1)} %get-tuple-element.7) | data formatting | bytes 24576
  59.2 1.3 %copy.18 = bf16[1,24,256]{2,1,0:T(8,128)(2,1)} copy(bf16[1,24,256]{2,1,0:T(8,128)(2,1)} %get-tuple-element.8) | data formatting | bytes 24576
